TPU v7x, 128 devices: a whole 4x4x4 slice. The times are simulated.
128 devices in a mesh: group: 4 (over z_lo, core), dp: 2 (over z_hi), tensor: 16 (over x, y).
Axes of the slice: x: 4, y: 4, z: 4 (z_hi: 2, z_lo: 2; z = z_hi * 2 + z_lo), core: 2. Of those that a mesh axis runs over, the one named last changes fastest.
Arguments:
- tokens: bfloat16 [2048, 8, 2048], P('tensor', ('group', 'dp')), may hold values from -6 to 6
- cotangent: bfloat16 [2048, 8, 2048], P('tensor', ('group', 'dp')), may hold values from -6 to 6
- lengths: int32 [8], replicated, may hold values from 1 to 2048, 9830 in all
- ln1_gain: float32 [2048], replicated, may hold values from 0.25 to 1.75
- ln1_bias: float32 [2048], replicated, may hold values from -1.75 to 1.75
- w_qkv: bfloat16 [2048, 3, 16, 128], P(None, None, 'tensor'), may hold values from -0.125 to 0.125
- b_qv: float32 [2, 2048], P(None, 'tensor'), may hold values from -1.75 to 1.75
- w_o: bfloat16 [16, 128, 2048], P('tensor'), may hold values from -0.75 to 0.75
- b_o: float32 [2048], replicated, may hold values from -1.75 to 1.75
- ln2_gain: float32 [2048], replicated, may hold values from 0.25 to 1.75
- ln2_bias: float32 [2048], replicated, may hold values from -1.75 to 1.75
- w_in: bfloat16 [2048, 8192], P(None, 'tensor'), may hold values from -0.125 to 0.125
- b_in: float32 [8192], P('tensor'), may hold values from -1.75 to 1.75
- w_out: bfloat16 [8192, 2048], P('tensor'), may hold values from -0.0625 to 0.0625
- b_out: float32 [2048], replicated, may hold values from -1.75 to 1.75
Outputs:
- output: bfloat16 [2048, 8, 2048], P('tensor', ('group', 'dp'))
- input_grad: bfloat16 [2048, 8, 2048], P('tensor', ('group', 'dp'))
- d_ln1_gain: float32 [2048], P(('group', 'dp', 'tensor'))
- d_ln1_bias: float32 [2048], P(('group', 'dp', 'tensor'))
- d_w_qkv: float32 [2048, 3, 16, 128], P(('group', 'dp'), None, 'tensor')
- d_b_qv: float32 [2, 2048], P(None, ('group', 'dp', 'tensor'))
- d_w_o: float32 [16, 128, 2048], P('tensor', None, ('group', 'dp'))
- d_b_o: float32 [2048], P(('group', 'dp', 'tensor'))
- d_ln2_gain: float32 [2048], P(('group', 'dp', 'tensor'))
- d_ln2_bias: float32 [2048], P(('group', 'dp', 'tensor'))
- d_w_in: float32 [2048, 8192], P(('group', 'dp'), 'tensor')
- d_b_in: float32 [8192], P(('group', 'dp', 'tensor'))
- d_w_out: float32 [8192, 2048], P('tensor', ('group', 'dp'))
- d_b_out: float32 [2048], P(('group', 'dp', 'tensor'))
Inputs may be any that keep to these rules, and one draw needn't show every extreme that they name: The true lengths of the 8 sequences sum to 9830.
All inputs are finite; a program needn't handle non-finite values.
Results may differ from a plain program's by a relative error of at most 0.02.
Values may be sent and summed in bfloat16 or wider, within the bound.
No kernel may reach another device: no remote copies, remote signals or barrier semaphores. Data moves between devices by JAX's collectives and lax.ppermute only.
A program may use at most 192 MiB of HBM per device.

v0:
```python
from functools import partial
import math
import jax
import jax.numpy as jnp
from jax import lax
from jax.sharding import PartitionSpec as P

EPS = 1e-05
NEGATIVE = -1e30


def layer_norm(value, gain, shift):
    mean = jnp.mean(value, axis=-1, keepdims=True)
    centred = value - mean
    spread = jnp.mean(centred * centred, axis=-1, keepdims=True)
    return centred * lax.rsqrt(spread + EPS) * gain + shift


def gelu_tanh(value):
    return jax.nn.gelu(value, approximate=True)


def block_scores(rows_query, key_rows, first, length, score_scale):
    count = rows_query.shape[0]
    key_pos = jnp.arange(key_rows.shape[0], dtype=jnp.int32)
    query_pos = first + jnp.arange(count, dtype=jnp.int32)
    valid = (key_pos[None, :] <= query_pos[:, None]) & (key_pos[None, :] < length)
    scores = (
        lax.dot_general(
            rows_query, key_rows, (((1,), (1,)), ((), ())), preferred_element_type=jnp.float32
        )
        * score_scale
    )
    return (jnp.where(valid, scores, NEGATIVE), valid)


def attend_forward(item, block_rows, score_scale):
    query, key_rows, value_rows, length = item
    outputs = []
    log_parts = []
    for first in range(0, query.shape[0], block_rows):
        rows_query = query[first : first + block_rows]
        scores, valid = block_scores(rows_query, key_rows, first, length, score_scale)
        peak = jnp.max(scores, axis=-1, keepdims=True)
        expo = jnp.exp(scores - peak)
        weight_sum = jnp.sum(expo, axis=-1, keepdims=True)
        probs = (expo / weight_sum).astype(jnp.bfloat16)
        outputs.append(
            jnp.dot(probs, value_rows, preferred_element_type=jnp.float32).astype(jnp.bfloat16)
        )
        log_parts.append((peak + jnp.log(weight_sum))[:, 0])
    return (jnp.concatenate(outputs, 0), jnp.concatenate(log_parts, 0))


def attend_backward(item, block_rows, score_scale):
    query, key_rows, value_rows, length, grad_out, log_sums = item
    key_grad = jnp.zeros(key_rows.shape, jnp.float32)
    value_grad = jnp.zeros(value_rows.shape, jnp.float32)
    query_parts = []
    for first in range(0, query.shape[0], block_rows):
        rows_query = query[first : first + block_rows]
        scores, valid = block_scores(rows_query, key_rows, first, length, score_scale)
        probs = jnp.where(valid, jnp.exp(scores - log_sums[first : first + block_rows, None]), 0.0)
        grad_rows = grad_out[first : first + block_rows]
        probs_grad = lax.dot_general(
            grad_rows, value_rows, (((1,), (1,)), ((), ())), preferred_element_type=jnp.float32
        )
        inner = jnp.sum(probs * probs_grad, axis=-1, keepdims=True)
        score_grad = (probs * (probs_grad - inner)).astype(jnp.bfloat16)
        query_parts.append(
            jnp.dot(score_grad, key_rows, preferred_element_type=jnp.float32) * score_scale
        )
        key_grad = (
            key_grad
            + lax.dot_general(
                score_grad, rows_query, (((0,), (0,)), ((), ())), preferred_element_type=jnp.float32
            )
            * score_scale
        )
        value_grad = value_grad + lax.dot_general(
            probs.astype(jnp.bfloat16),
            grad_rows,
            (((0,), (0,)), ((), ())),
            preferred_element_type=jnp.float32,
        )
    return (
        jnp.concatenate(query_parts, 0).astype(jnp.bfloat16),
        key_grad.astype(jnp.bfloat16),
        value_grad.astype(jnp.bfloat16),
    )


def shards(
    tokens,
    cotangent,
    lengths,
    ln1_gain,
    ln1_bias,
    w_qkv,
    b_qv,
    w_o,
    b_o,
    ln2_gain,
    ln2_bias,
    w_in,
    b_in,
    w_out,
    b_out,
):
    row_count, seq_count, model_width = tokens.shape
    tensor_count = lax.axis_size("tensor")
    tensor_rank = lax.axis_index("tensor")
    seq_total = row_count * tensor_count
    local_heads = w_qkv.shape[2]
    head_size = w_qkv.shape[3]
    local_width = local_heads * head_size
    hidden = w_in.shape[1]
    block_rows = min(512, seq_total)
    score_scale = 1.0 / math.sqrt(head_size)
    group_count = lax.axis_size("group")
    group_rank = lax.axis_index("group")
    member = group_rank * lax.axis_size("dp") + lax.axis_index("dp")
    seq_lengths = lax.dynamic_slice_in_dim(lengths, member * seq_count, seq_count, 0)
    group_totals = jnp.sum(lengths.reshape(group_count, -1), axis=1).astype(jnp.float32)
    factor = (
        group_count
        * lax.dynamic_index_in_dim(group_totals, group_rank, 0, keepdims=False)
        / jnp.sum(group_totals)
    )
    inputs = tokens.astype(jnp.float32)
    normed_low = layer_norm(inputs, ln1_gain, ln1_bias).astype(jnp.bfloat16)
    normed_full = lax.all_gather(normed_low, "tensor", axis=0, tiled=True)
    joint_weight = w_qkv.reshape(model_width, 3 * local_width)
    projected = jnp.dot(
        normed_full.reshape(seq_total * seq_count, model_width),
        joint_weight,
        preferred_element_type=jnp.float32,
    )
    projected = projected.reshape(seq_total, seq_count, 3, local_width)
    query = (projected[:, :, 0] + b_qv[0]).astype(jnp.bfloat16)
    keys = projected[:, :, 1].astype(jnp.bfloat16)
    values = (projected[:, :, 2] + b_qv[1]).astype(jnp.bfloat16)

    def per_item(array):
        shaped = array.reshape(seq_total, seq_count, local_heads, head_size)
        return jnp.transpose(shaped, (1, 2, 0, 3)).reshape(
            seq_count * local_heads, seq_total, head_size
        )

    def per_row(array):
        shaped = array.reshape(seq_count, local_heads, seq_total, head_size)
        return jnp.transpose(shaped, (2, 0, 1, 3)).reshape(seq_total, seq_count, local_width)

    query_items = per_item(query)
    key_items = per_item(keys)
    value_items = per_item(values)
    item_lengths = jnp.repeat(seq_lengths, local_heads)
    heads_out, log_sums = lax.map(
        partial(attend_forward, block_rows=block_rows, score_scale=score_scale),
        (query_items, key_items, value_items, item_lengths),
    )
    attended = per_row(heads_out)
    out_weight = w_o.reshape(local_width, model_width)
    piece = attended
    attention = (
        lax.psum_scatter(
            jnp.einsum("rse,ed->rsd", piece, out_weight, preferred_element_type=jnp.float32),
            "tensor",
            scatter_dimension=0,
            tiled=True,
        )
        + b_o
    )
    middle = inputs + attention
    second_low = layer_norm(middle, ln2_gain, ln2_bias).astype(jnp.bfloat16)
    second_full = lax.all_gather(second_low, "tensor", axis=0, tiled=True)
    pre_act = (
        jnp.dot(
            second_full.reshape(seq_total * seq_count, model_width),
            w_in,
            preferred_element_type=jnp.float32,
        )
        + b_in
    )
    activated = gelu_tanh(pre_act).astype(jnp.bfloat16).reshape(seq_total, seq_count, hidden)
    piece = activated
    feed = (
        lax.psum_scatter(
            jnp.einsum("rsf,fd->rsd", piece, w_out, preferred_element_type=jnp.float32).astype(
                jnp.bfloat16
            ),
            "tensor",
            scatter_dimension=0,
            tiled=True,
        ).astype(jnp.float32)
        + b_out
    )
    output = (middle + feed).astype(jnp.bfloat16)
    positions = tensor_rank * row_count + jnp.arange(row_count, dtype=jnp.int32)
    live = positions[:, None] < seq_lengths[None, :]
    upstream = jnp.where(live[:, :, None], cotangent, jnp.zeros_like(cotangent))
    piece = lax.all_gather(upstream, "tensor", axis=0, tiled=True)
    weight_grad = jnp.einsum("rsf,rsd->fd", activated, piece, preferred_element_type=jnp.float32)
    part = jnp.einsum("rsd,fd->rsf", piece, w_out, preferred_element_type=jnp.float32)
    act_grad = part
    grad_w_out = weight_grad
    gelu_back = jax.vjp(gelu_tanh, pre_act)[1]
    pre_low = gelu_back(act_grad.reshape(seq_total * seq_count, hidden))[0].astype(jnp.bfloat16)
    grad_b_in = jnp.sum(pre_low, axis=0, dtype=jnp.float32)
    grad_w_in = jnp.einsum(
        "rd,rf->df",
        second_full.reshape(seq_total * seq_count, model_width),
        pre_low,
        preferred_element_type=jnp.float32,
    )
    pre_rows = pre_low.reshape(seq_total, seq_count, hidden)
    piece = pre_rows
    second_grad = lax.psum_scatter(
        jnp.einsum("rsf,df->rsd", piece, w_in, preferred_element_type=jnp.float32),
        "tensor",
        scatter_dimension=0,
        tiled=True,
    )
    norm_two_back = jax.vjp(layer_norm, middle, ln2_gain, ln2_bias)[1]
    middle_part, grad_ln2_gain, grad_ln2_bias = norm_two_back(second_grad)
    middle_grad = upstream.astype(jnp.float32) + middle_part
    branch_low = middle_grad.astype(jnp.bfloat16)
    grad_b_o = jnp.sum(branch_low, axis=(0, 1), dtype=jnp.float32)
    grad_b_out = jnp.sum(upstream, axis=(0, 1), dtype=jnp.float32)
    piece = lax.all_gather(branch_low, "tensor", axis=0, tiled=True)
    weight_grad = jnp.einsum("rse,rsd->ed", attended, piece, preferred_element_type=jnp.float32)
    part = jnp.einsum("rsd,ed->rse", piece, out_weight, preferred_element_type=jnp.float32)
    head_items = per_item(part.astype(jnp.bfloat16))
    grads_query, grads_keys, grads_values = lax.map(
        partial(attend_backward, block_rows=block_rows, score_scale=score_scale),
        (query_items, key_items, value_items, item_lengths, head_items, log_sums),
    )
    joint_grad = jnp.stack(
        (per_row(grads_query), per_row(grads_keys), per_row(grads_values)), axis=2
    )
    grad_b_qv = jnp.sum(joint_grad[:, :, 0::2], axis=(0, 1), dtype=jnp.float32)
    joint_rows = joint_grad.reshape(seq_total, seq_count, 3 * local_width)
    grad_w_qkv = jnp.einsum(
        "rd,rc->dc",
        normed_full.reshape(seq_total * seq_count, model_width),
        joint_rows.reshape(seq_total * seq_count, 3 * local_width),
        preferred_element_type=jnp.float32,
    )
    piece = joint_rows
    normed_grad = lax.psum_scatter(
        jnp.einsum("rsc,dc->rsd", piece, joint_weight, preferred_element_type=jnp.float32).astype(
            jnp.bfloat16
        ),
        "tensor",
        scatter_dimension=0,
        tiled=True,
    ).astype(jnp.float32)
    norm_one_back = jax.vjp(layer_norm, inputs, ln1_gain, ln1_bias)[1]
    input_part, grad_ln1_gain, grad_ln1_bias = norm_one_back(normed_grad)
    input_grad = (middle_grad + input_part).astype(jnp.bfloat16)
    matrices = (
        grad_w_qkv.reshape(model_width, 3, local_heads, head_size) * factor,
        weight_grad.reshape(local_heads, head_size, model_width) * factor,
        grad_w_in * factor,
        grad_w_out * factor,
    )
    summed = (
        lax.psum_scatter(
            matrices[0].astype(jnp.bfloat16), ("group", "dp"), scatter_dimension=0, tiled=True
        ).astype(jnp.float32),
        lax.psum_scatter(
            matrices[1].astype(jnp.bfloat16), ("group", "dp"), scatter_dimension=2, tiled=True
        ).astype(jnp.float32),
        lax.psum_scatter(
            matrices[2].astype(jnp.bfloat16), ("group", "dp"), scatter_dimension=0, tiled=True
        ).astype(jnp.float32),
        lax.psum_scatter(
            matrices[3].astype(jnp.bfloat16), ("group", "dp"), scatter_dimension=1, tiled=True
        ).astype(jnp.float32),
    )
    in_full = lax.dynamic_update_slice_in_dim(
        jnp.zeros((hidden * tensor_count,), jnp.float32), grad_b_in, tensor_rank * hidden, 0
    )
    joint_full = lax.dynamic_update_slice_in_dim(
        jnp.zeros((2, local_width * tensor_count), jnp.float32),
        grad_b_qv,
        tensor_rank * local_width,
        1,
    )
    stacked = (
        jnp.concatenate(
            (
                jnp.stack(
                    (
                        grad_ln1_gain,
                        grad_ln1_bias,
                        grad_b_o,
                        grad_ln2_gain,
                        grad_ln2_bias,
                        grad_b_out,
                    )
                ),
                joint_full,
            ),
            0,
        )
        * factor
    )
    vector_sums, in_sums = (
        lax.psum_scatter(stacked, ("group", "dp", "tensor"), scatter_dimension=1, tiled=True),
        lax.psum_scatter(
            in_full * factor, ("group", "dp", "tensor"), scatter_dimension=0, tiled=True
        ),
    )
    return (
        output,
        input_grad,
        vector_sums[0],
        vector_sums[1],
        summed[0],
        vector_sums[6:8],
        summed[1],
        vector_sums[2],
        vector_sums[3],
        vector_sums[4],
        summed[2],
        in_sums,
        summed[3],
        vector_sums[5],
    )


def solution(mesh):
    in_specs = (
        P("tensor", ("group", "dp"), None),
        P("tensor", ("group", "dp"), None),
        P(),
        P(),
        P(),
        P(None, None, "tensor", None),
        P(None, "tensor"),
        P("tensor", None, None),
        P(),
        P(),
        P(),
        P(None, "tensor"),
        P("tensor"),
        P("tensor", None),
        P(),
    )
    out_specs = (
        P("tensor", ("group", "dp"), None),
        P("tensor", ("group", "dp"), None),
        P(("group", "dp", "tensor")),
        P(("group", "dp", "tensor")),
        P(("group", "dp"), None, "tensor", None),
        P(None, ("group", "dp", "tensor")),
        P("tensor", None, ("group", "dp")),
        P(("group", "dp", "tensor")),
        P(("group", "dp", "tensor")),
        P(("group", "dp", "tensor")),
        P(("group", "dp"), "tensor"),
        P(("group", "dp", "tensor")),
        P("tensor", ("group", "dp")),
        P(("group", "dp", "tensor")),
    )
    return jax.shard_map(shards, mesh=mesh, in_specs=in_specs, out_specs=out_specs, check_vma=False)
```

profile of v0, /device:TPU:96, one launch (start us, length us, event | category | flops | bytes accessed | tf_op | source)
XLA Modules:
  0.0 1723.6 jit_solution(11324964571885417214)
XLA Ops:
  7.3 1.3 convert_reduce_fusion.3
  8.6 1.3 fusion.81
  10.5 2.3 fusion.80
  12.8 2.6 copy.51
  16.8 68.1 %all-gather.5.cloned.1.call-done = bf16[2048,1,2048]{2,0,1:T(8,128)(2,1)} async-done(((bf16[128,1,2048]{2,0,1:T(8,128)(2,1)}), bf16[2048,1,2048]{2,0,1:T(8,128)(2,1)}) %all-gather.5.cloned.1.call-update) | async-done | bytes 8388624 | tf_op jit(solution)/shard_map/all_gather | solution.py:132
  84.8 7.4 fusion.31
  93.6 3.6 fusion.113
  97.1 3.9 fusion.116
  101.0 4.0 online-softmax.3
  106.0 5.1 fusion.115
  111.1 4.0 online-softmax.2
  116.1 5.1 fusion.114
  121.1 4.0 online-softmax.1
  126.2 4.4 online-softmax
  132.2 8.1 convolution_bitcast_fusion.1
  140.4 110.3 %reduce-scatter.12.cloned.1.call-done = f32[128,1,2048]{2,0,1:T(8,128)} async-done(((f32[2048,1,2048]{2,0,1:T(8,128)}), f32[128,1,2048]{2,0,1:T(8,128)}) %reduce-scatter.12.cloned.1.call-update) | async-done | bytes 1048592 | tf_op jit(solution)/shard_map/reduce_scatter | solution.py:166
  250.7 1.6 fusion.111
  253.6 1.7 add_convert_fusion.3
  256.1 2.6 convert_reduce_fusion.4
  258.8 67.0 %all-gather.7.cloned.1.call-done = bf16[2048,1,2048]{2,0,1:T(8,128)(2,1)} async-done(((bf16[128,1,2048]{2,0,1:T(8,128)(2,1)}), bf16[2048,1,2048]{2,0,1:T(8,128)(2,1)}) %all-gather.7.cloned.1.call-update) | async-done | bytes 8388624 | tf_op jit(solution)/shard_map/all_gather | solution.py:176
  325.7 10.5 fusion.10
  336.2 62.4 %all-gather.9.cloned.1.call-done = bf16[2048,1,2048]{2,0,1:T(8,128)(2,1)} async-done(((bf16[128,1,2048]{2,0,1:T(8,128)(2,1)}), bf16[2048,1,2048]{2,0,1:T(8,128)(2,1)}) %all-gather.9.cloned.1.call-update) | async-done | bytes 8388624 | tf_op jit(solution)/shard_map/all_gather | solution.py:202
  398.7 12.4 convert_reduce_fusion
  411.1 1.4 copy-done.72
  412.5 8.2 convolution_bitcast_fusion
  420.8 10.3 convert_bitcast_fusion.1
  431.2 99.9 %reduce-scatter.16.cloned.1.call-done = f32[128,1,2048]{2,0,1:T(8,128)} async-done(((f32[2048,1,2048]{2,0,1:T(8,128)}), f32[128,1,2048]{2,0,1:T(8,128)}) %reduce-scatter.16.cloned.1.call-update) | async-done | bytes 1048592 | tf_op jit(solution)/shard_map/reduce_scatter | solution.py:218
  531.1 2.2 multiply_reduce_fusion.4
  533.3 85.7 %reduce-scatter.14.cloned.1.call-done = bf16[128,1,2048]{2,0,1:T(8,128)(2,1)} async-done(((bf16[2048,1,2048]{2,0,1:T(8,128)(2,1)}), bf16[128,1,2048]{2,0,1:T(8,128)(2,1)}) %reduce-scatter.14.cloned.1.call-update) | async-done | bytes 524304 | tf_op jit(solution)/shard_map/reduce_scatter | solution.py:188
  619.0 2.5 fusion.110
  625.8 11.3 multiply_convert_fusion
  637.2 3.1 exponential_reduce_fusion
  645.5 9.6 multiply_convert_fusion.1
  655.6 37.3 %all-gather.11.cloned.1.call-done = bf16[2048,1,2048]{2,0,1:T(8,128)(2,1)} async-done(((bf16[128,1,2048]{2,0,1:T(8,128)(2,1)}), bf16[2048,1,2048]{2,0,1:T(8,128)(2,1)}) %all-gather.11.cloned.1.call-update) | async-done | bytes 8388624 | tf_op jit(solution)/shard_map/all_gather | solution.py:230
  692.9 5.9 fusion.45
  698.8 2.8 fusion.97
  701.7 2.9 fusion.100
  704.6 2.7 fusion.103
  708.0 9.5 multiply_reduce_fusion
  717.5 4.5 multiply_convert_fusion.3
  722.1 9.5 multiply_convert_fusion.2
  731.6 2.1 fusion.75
  733.7 3.3 fusion.77
  737.0 1.4 fusion.78
  738.4 1.4 fusion.76
  743.7 1.7 convolution_add_fusion.2
  745.5 1.7 convolution_add_fusion.1
  747.2 2.8 fusion.56
  750.0 2.3 fusion.53
  753.6 1.6 copy.60
  755.2 8.3 fusion.38
  763.6 9.7 convert_bitcast_fusion
  774.1 75.9 %all-reduce = f32[8192]{0:T(1024)S(1)} all-reduce(f32[8192]{0:T(1024)S(1)} %broadcast_multiply_fusion.1), channel_id=10, replica_groups=mesh['group'=4,'dp'=2,'tensor'=16] {'group','dp','tensor'}, use_global_device_ids=true, to_apply=%region_38.39.clone | all-reduce | flops 8192 | bytes 65536
  850.6 1.8 convert_element_type.264
  852.4 1.8 convert_element_type.261
  855.4 1.7 convert_element_type.259
  857.0 45.5 %reduce-scatter.20.cloned.1.call-done = bf16[256,3,1,128]{3,0,1,2:T(8,128)(2,1)} async-done(((bf16[2048,3,1,128]{3,0,1,2:T(8,128)(2,1)}), bf16[256,3,1,128]{3,0,1,2:T(8,128)(2,1)}) %reduce-scatter.20.cloned.1.call-update) | async-done | bytes 196624 | tf_op jit(solution)/shard_map/reduce_scatter | solution.py:268
  902.5 2.0 copy.62
  904.5 90.2 %reduce-scatter.18.cloned.1.call-done = bf16[128,1,2048]{2,0,1:T(8,128)(2,1)} async-done(((bf16[2048,1,2048]{2,0,1:T(8,128)(2,1)}), bf16[128,1,2048]{2,0,1:T(8,128)(2,1)}) %reduce-scatter.18.cloned.1.call-update) | async-done | bytes 524304 | tf_op jit(solution)/shard_map/reduce_scatter | solution.py:250
  994.7 1.4 convert_reduce_fusion.2
  996.1 1.6 fusion.83
  997.9 1.3 copy.73
  999.2 2.7 add_convert_fusion
  1002.0 709.0 %reduce-scatter.28.cloned.1.call-done = f32[16,8]{1,0:T(8,128)} async-done(((f32[2048,8]{1,0:T(8,128)}), f32[16,8]{1,0:T(8,128)}) %reduce-scatter.28.cloned.1.call-update) | async-done | bytes 528
  (239 shorter events, 33.2 us)
Async XLA Ops:
  7.2 391.5 %copy-start = (bf16[512,2048]{1,0:T(8,128)(2,1)S(1)}, bf16[512,2048]{1,0:T(8,128)(2,1)}, u32[]{:S(2)}) copy-start(bf16[512,2048]{1,0:T(8,128)(2,1)} %param.28) | copy-start | bytes 6291460
  7.2 8.3 copy-start.66
  7.2 9.5 copy-start.63
  7.2 77.6 %all-gather.5.cloned.1.call-start = ((), (), s32[]{:S(2)}) async-start(), calls=%async_computation.9 | async-start | bytes 8912896 | tf_op jit(solution)/shard_map/all_gather | solution.py:132
  9.9 82.3 %copy-start.68 = (f32[128]{0:T(128)}, f32[128]{0:T(128)S(1)}, u32[]{:S(2)}) copy-start(f32[128]{0:T(128)S(1)} %fusion.81) | copy-start | bytes 1540
  12.8 237.9 %reduce-scatter.12.cloned.1.call-start = ((), (), s32[]{:S(2)}) async-start(), calls=%async_computation.10 | async-start | bytes 17825792 | tf_op jit(solution)/shard_map/reduce_scatter | solution.py:166
  16.0 100.0 %copy-start.35 = (s32[512]{0:T(512)}, s32[512]{0:T(512)S(1)}, u32[]{:S(2)}) copy-start(s32[512]{0:T(512)S(1)} %iota_add_fusion.2) | copy-start | bytes 6148
  16.0 89.9 %copy-start.33 = (s32[512]{0:T(512)}, s32[512]{0:T(512)S(1)}, u32[]{:S(2)}) copy-start(s32[512]{0:T(512)S(1)} %iota_add_fusion.1) | copy-start | bytes 6148
  16.7 75.6 %copy-start.56 = (f32[128]{0:T(128)}, f32[128]{0:T(128)S(1)}, u32[]{:S(2)}) copy-start(f32[128]{0:T(128)S(1)} %get-tuple-element.136) | copy-start | bytes 1540
  92.2 4.9 copy-start.12
  92.3 23.7 %copy-start.17 = (bf16[2048,1,128]{2,0,1:T(8,128)(2,1)}, bf16[2048,1,128]{2,0,1:T(8,128)(2,1)S(1)}, u32[]{:S(2)}) copy-start(bf16[2048,1,128]{2,0,1:T(8,128)(2,1)S(1)} %fusion.85) | copy-start | bytes 1572868
  125.1 7.1 copy-start.23
  140.3 113.3 %copy-start.29 = (f32[2048]{0:T(1024)S(1)}, f32[2048]{0:T(1024)}, u32[]{:S(2)}) copy-start(f32[2048]{0:T(1024)} %param.24) | copy-start | bytes 24580
  140.3 185.4 %all-gather.7.cloned.1.call-start = ((), (), s32[]{:S(2)}) async-start(), calls=%async_computation.11 | async-start | bytes 8912896 | tf_op jit(solution)/shard_map/all_gather | solution.py:176
  255.3 143.3 %all-gather.9.cloned.1.call-start = ((), (), s32[]{:S(2)}) async-start(), calls=%async_computation.13 | async-start | bytes 8912896 | tf_op jit(solution)/shard_map/all_gather | solution.py:202
  258.7 272.4 %reduce-scatter.16.cloned.1.call-start = ((), (), s32[]{:S(2)}) async-start(), calls=%async_computation.14 | async-start | bytes 17825792 | tf_op jit(solution)/shard_map/reduce_scatter | solution.py:218
  398.7 13.8 copy-start.70
  420.7 198.3 %reduce-scatter.14.cloned.1.call-start = ((), (), s32[]{:S(2)}) async-start(), calls=%async_computation.12 | async-start | bytes 8912896 | tf_op jit(solution)/shard_map/reduce_scatter | solution.py:188
  431.0 100.0 %copy-start.53 = (f32[128]{0:T(128)S(1)}, f32[128]{0:T(128)}, u32[]{:S(2)}) copy-start(f32[128]{0:T(128)} %copy-done.52) | copy-start | bytes 1540
  431.0 100.0 %copy-start.59 = (f32[128]{0:T(128)S(1)}, f32[128]{0:T(128)}, u32[]{:S(2)}) copy-start(f32[128]{0:T(128)} %copy-done.58) | copy-start | bytes 1540
  431.0 102.2 %copy-start.65 = (f32[128]{0:T(128)S(1)}, f32[128]{0:T(128)}, u32[]{:S(2)}) copy-start(f32[128]{0:T(128)} %copy-done.64) | copy-start | bytes 1540
  431.0 188.0 %copy-start.51 = (f32[2048]{0:T(1024)S(1)}, f32[2048]{0:T(1024)}, u32[]{:S(2)}) copy-start(f32[2048]{0:T(1024)} %param.29) | copy-start | bytes 24580
  431.1 190.5 %copy-start.15 = (bf16[128,1,2048]{2,0,1:T(8,128)(2,1)S(1)}, bf16[128,1,2048]{2,0,1:T(8,128)(2,1)}, u32[]{:S(2)}) copy-start(bf16[128,1,2048]{2,0,1:T(8,128)(2,1)} %get-tuple-element.119) | copy-start | bytes 1572868
  431.1 191.9 %copy-start.67 = (s32[8]{0:T(128)S(1)}, s32[8]{0:T(128)}, u32[]{:S(2)}) copy-start(s32[8]{0:T(128)} %param.17) | copy-start | bytes 100
  431.1 194.6 %copy-start.71 = (f32[512]{0:T(512)S(1)}, f32[512]{0:T(512)}, u32[]{:S(2)}) copy-start(f32[512]{0:T(512)} %param.27) | copy-start | bytes 6148
  431.1 261.8 %all-gather.11.cloned.1.call-start = ((), (), s32[]{:S(2)}) async-start(), calls=%async_computation.15 | async-start | bytes 8912896 | tf_op jit(solution)/shard_map/all_gather | solution.py:230
  621.6 15.5 copy-start.14
  621.6 15.5 copy-start.60
  622.7 227.9 %reduce-scatter.26.cloned.1.call-start = ((), (), s32[]{:S(2)}) async-start(), calls=%async_computation.20 | async-start | bytes 2359296 | tf_op jit(solution)/shard_map/reduce_scatter | solution.py:277
  625.7 11.4 copy-start.48
  637.1 215.3 %reduce-scatter.24.cloned.1.call-start = ((), (), s32[]{:S(2)}) async-start(), calls=%async_computation.19 | async-start | bytes 2359296 | tf_op jit(solution)/shard_map/reduce_scatter | solution.py:274
  637.1 4.9 copy-start.5
  637.1 4.9 copy-start.49
  641.4 76.1 %copy-start.39 = (f32[512]{0:T(512)}, f32[512]{0:T(512)S(1)}, u32[]{:S(2)}) copy-start(f32[512]{0:T(512)S(1)} %get-tuple-element.150) | copy-start | bytes 6148
  641.4 80.6 %copy-start.37 = (f32[512]{0:T(512)}, f32[512]{0:T(512)S(1)}, u32[]{:S(2)}) copy-start(f32[512]{0:T(512)S(1)} %get-tuple-element.149) | copy-start | bytes 6148
  644.2 77.9 %copy-start.41 = (f32[512]{0:T(512)}, f32[512]{0:T(512)S(1)}, u32[]{:S(2)}) copy-start(f32[512]{0:T(512)S(1)} %get-tuple-element.151) | copy-start | bytes 6148
  644.2 77.9 %copy-start.43 = (f32[512]{0:T(512)}, f32[512]{0:T(512)S(1)}, u32[]{:S(2)}) copy-start(f32[512]{0:T(512)S(1)} %get-tuple-element.152) | copy-start | bytes 6148
  645.5 47.4 %copy-start.24 = (bf16[1,128,2048]{2,1,0:T(8,128)(2,1)S(1)}, bf16[1,128,2048]{2,1,0:T(8,128)(2,1)}, u32[]{:S(2)}) copy-start(bf16[1,128,2048]{2,1,0:T(8,128)(2,1)} %param.22) | copy-start | bytes 1572868
  655.2 200.2 %reduce-scatter.22.cloned.1.call-start = ((), (), s32[]{:S(2)}) async-start(), calls=%async_computation.18 | async-start | bytes 589824 | tf_op jit(solution)/shard_map/reduce_scatter | solution.py:271
  692.9 14.3 copy-start.8
  698.8 8.4 copy-start.21
  698.8 8.4 copy-start.6
  701.7 5.6 copy-start.2
  701.7 6.3 copy-start.4
  701.7 6.3 copy-start.34
  701.7 6.3 copy-start.36
  731.6 5.4 copy-start.13
  731.6 6.8 copy-start.11
  733.7 6.1 copy-start.18
  745.4 4.5 slice-start
  752.4 150.2 %reduce-scatter.20.cloned.1.call-start = ((), (), s32[]{:S(2)}) async-start(), calls=%async_computation.17 | async-start | bytes 1769472 | tf_op jit(solution)/shard_map/reduce_scatter | solution.py:268
  763.6 231.1 %reduce-scatter.18.cloned.1.call-start = ((), (), s32[]{:S(2)}) async-start(), calls=%async_computation.16 | async-start | bytes 8912896 | tf_op jit(solution)/shard_map/reduce_scatter | solution.py:250
  773.3 221.4 %copy-start.9 = (bf16[128,1,2048]{2,0,1:T(8,128)(2,1)S(1)}, bf16[128,1,2048]{2,0,1:T(8,128)(2,1)}, u32[]{:S(2)}) copy-start(bf16[128,1,2048]{2,0,1:T(8,128)(2,1)} %param.15) | copy-start | bytes 1572868
  773.3 221.4 %copy-start.28 = (f32[2048]{0:T(1024)S(1)}, f32[2048]{0:T(1024)}, u32[]{:S(2)}) copy-start(f32[2048]{0:T(1024)} %param.18) | copy-start | bytes 24580
  773.3 221.4 %copy-start.46 = (f32[128]{0:T(128)S(1)}, f32[128]{0:T(128)}, u32[]{:S(2)}) copy-start(f32[128]{0:T(128)} %copy-done.45) | copy-start | bytes 1540
  773.3 222.8 %copy-start.69 = (f32[128]{0:T(128)S(1)}, f32[128]{0:T(128)}, u32[]{:S(2)}) copy-start(f32[128]{0:T(128)} %copy-done.68) | copy-start | bytes 1540
  773.3 222.8 %copy-start.55 = (f32[128]{0:T(128)S(1)}, f32[128]{0:T(128)}, u32[]{:S(2)}) copy-start(f32[128]{0:T(128)} %copy-done.54) | copy-start | bytes 1540
  773.3 224.4 %copy-start.30 = (f32[2048]{0:T(1024)S(1)}, f32[2048]{0:T(1024)}, u32[]{:S(2)}) copy-start(f32[2048]{0:T(1024)} %get-tuple-element.118) | copy-start | bytes 24580
  773.3 224.4 %copy-start.31 = (f32[2048]{0:T(1024)S(1)}, f32[2048]{0:T(1024)}, u32[]{:S(2)}) copy-start(f32[2048]{0:T(1024)} %get-tuple-element.107) | copy-start | bytes 24580
  773.4 224.4 %copy-start.32 = (f32[2048]{0:T(1024)S(1)}, f32[2048]{0:T(1024)}, u32[]{:S(2)}) copy-start(f32[2048]{0:T(1024)} %get-tuple-element.111) | copy-start | bytes 24580
  773.4 225.9 %copy-start.16 = (bf16[128,1,2048]{2,0,1:T(8,128)(2,1)S(1)}, bf16[128,1,2048]{2,0,1:T(8,128)(2,1)}, u32[]{:S(2)}) copy-start(bf16[128,1,2048]{2,0,1:T(8,128)(2,1)} %get-tuple-element.119) | copy-start | bytes 1572868
  773.4 225.9 %copy-start.61 = (f32[128]{0:T(128)S(1)}, f32[128]{0:T(128)}, u32[]{:S(2)}) copy-start(f32[128]{0:T(128)} %copy-done.60) | copy-start | bytes 1540
  773.4 937.6 %reduce-scatter.28.cloned.1.call-start = ((), (), s32[]{:S(2)}) async-start(), calls=%async_computation.21 | async-start | bytes 1056768
  855.4 861.5 %copy-start.1 = (bf16[512,2048]{1,0:T(8,128)(2,1)S(1)}, bf16[512,2048]{1,0:T(8,128)(2,1)}, u32[]{:S(2)}) copy-start(bf16[512,2048]{1,0:T(8,128)(2,1)} %param.28) | copy-start | bytes 6291460
  (25 other events, 46.6 us)
Sparse Core Ops, SparseCore 0:
  12.9 71.8 all-gather.4
  140.5 110.1 reduce-scatter.11
  255.5 70.2 all-gather.6
  328.3 70.3 all-gather.8
  420.8 110.1 reduce-scatter.15
  534.3 84.6 reduce-scatter.13
  622.8 70.0 all-gather.10
  695.3 56.2 reduce-scatter.25
  754.1 60.7 reduce-scatter.23
  817.0 38.2 reduce-scatter.21
  857.9 44.5 reduce-scatter.19
  906.2 88.4 reduce-scatter.17
  999.3 711.5 reduce-scatter.27
where the time goes:
time: 1730 us; the launch traced here: 1720 us
  waiting for transfers between devices  1380 us (80%)
  matrix products  158 us (9%)
  blocking collectives  75.9 us (4%)
  other arithmetic  57.2 us (3%)
  local copies, waits for them, and re-layouts  22.4 us (1%)
    unnamed x14, waiting for transfers between devices  709 us
    reduce_scatter x1, waiting for transfers between devices, shards(): lax.psum_scatter(jnp.einsum('rse,ed->rsd', piece, out_weight, preferred_e...  110 us
    reduce_scatter x1, waiting for transfers between devices, shards(): lax.psum_scatter(jnp.einsum('rsf,df->rsd', piece, w_in, preferred_element...  99.9 us
    reduce_scatter x1, waiting for transfers between devices, shards(): lax.psum_scatter(jnp.einsum('rsc,dc->rsd', piece, joint_weight, preferred...  90.2 us
    reduce_scatter x1, waiting for transfers between devices, shards(): lax.psum_scatter(jnp.einsum('rsf,fd->rsd', piece, w_out, preferred_elemen...  85.7 us
    unnamed x1, blocking collectives  75.9 us
    all_gather x1, waiting for transfers between devices, shards(): normed_full = lax.all_gather(normed_low, 'tensor', axis=0, tiled=True)  68.1 us
    all_gather x1, waiting for transfers between devices, shards(): second_full = lax.all_gather(second_low, 'tensor', axis=0, tiled=True)  67 us
  transfers between devices with their start and end apart: 13, of which 11 were waited for; matrix products, arithmetic and copies ran while one was open for 9% of the time, Pallas kernels for 0%

commit v1 on v0

--- a/solution.py
+++ b/solution.py
@@ -7,6 +7,12 @@
 
 EPS = 1e-05
 NEGATIVE = -1e30
+
+
+def gather_by_exchange(x, axis, dim):
+    size = lax.axis_size(axis)
+    repeats = [size if d == dim else 1 for d in range(x.ndim)]
+    return lax.all_to_all(jnp.tile(x, repeats), axis, split_axis=dim, concat_axis=dim, tiled=True)
 
 
 def layer_norm(value, gain, shift):
@@ -129,7 +135,7 @@
     )
     inputs = tokens.astype(jnp.float32)
     normed_low = layer_norm(inputs, ln1_gain, ln1_bias).astype(jnp.bfloat16)
-    normed_full = lax.all_gather(normed_low, "tensor", axis=0, tiled=True)
+    normed_full = gather_by_exchange(normed_low, "tensor", 0)
     joint_weight = w_qkv.reshape(model_width, 3 * local_width)
     projected = jnp.dot(
         normed_full.reshape(seq_total * seq_count, model_width),

time: 1730 us -> 1870 us (1.081)
  local copies, waits for them, and re-layouts: 22.4 us -> 98 us
  waiting for transfers between devices: 1380 us -> 1410 us
    all_to_all x0 -> x1, waiting for transfers between devices: none -> 143 us  [gather_by_exchange(): lax.all_to_all(jnp.tile(x, repeats), axis, split_axis=dim, concat_axis=di...]
    all_gather x1 -> x0, waiting for transfers between devices: 68.1 us -> none  [shards(): normed_full = lax.all_gather(normed_low, 'tensor', axis=0, tiled=True)]
    reshape x0 -> x1, local copies, waits for them, and re-layouts: none -> 39.2 us  [shards(): normed_full.reshape(seq_total * seq_count, model_width)]
    all_gather x1, waiting for transfers between devices: 37.3 us -> 0.02 us  [shards(): piece = lax.all_gather(branch_low, 'tensor', axis=0, tiled=True)]
    unnamed x163 -> x165, local copies, waits for them, and re-layouts: 17.5 us -> 49 us
    unnamed x14 -> x13, waiting for transfers between devices: 709 us -> 707 us
  transfers between devices with their start and end apart: 13 -> 13, of which waited for: 11 -> 10; matrix products, arithmetic and copies ran while one was open for 9% -> 10% of each run, Pallas kernels for 0% -> 0%
where the time goes in v1:
time: 1870 us; the launch traced here: 1860 us
  waiting for transfers between devices  1410 us (75%)
  matrix products  163 us (9%)
  local copies, waits for them, and re-layouts  98 us (5%)
  blocking collectives  73.7 us (4%)
  other arithmetic  69.1 us (4%)
    unnamed x13, waiting for transfers between devices  707 us
    all_to_all x1, waiting for transfers between devices, gather_by_exchange(): lax.all_to_all(jnp.tile(x, repeats), axis, split_axis=dim, concat_axis=di...  143 us
    reduce_scatter x1, waiting for transfers between devices, shards(): lax.psum_scatter(jnp.einsum('rse,ed->rsd', piece, out_weight, preferred_e...  113 us
    reduce_scatter x1, waiting for transfers between devices, shards(): lax.psum_scatter(jnp.einsum('rsf,df->rsd', piece, w_in, preferred_element...  99.9 us
    reduce_scatter x1, waiting for transfers between devices, shards(): lax.psum_scatter(jnp.einsum('rsc,dc->rsd', piece, joint_weight, preferred...  89.8 us
    reduce_scatter x1, waiting for transfers between devices, shards(): lax.psum_scatter(jnp.einsum('rsf,fd->rsd', piece, w_out, preferred_elemen...  85.8 us
    unnamed x1, blocking collectives  73.7 us
    all_gather x1, waiting for transfers between devices, shards(): second_full = lax.all_gather(second_low, 'tensor', axis=0, tiled=True)  67 us
  transfers between devices with their start and end apart: 13, of which 10 were waited for; matrix products, arithmetic and copies ran while one was open for 10% of the time, Pallas kernels for 0%

profile of v1, /device:TPU:96, one launch (start us, length us, event | category | flops | bytes accessed | tf_op | source)
XLA Modules:
  0.0 1859.6 jit_solution(11648446915370937903)
XLA Ops:
  10.9 1.5 fusion.91
  12.4 4.3 tile.12
  17.2 12.4 reduce.12
  29.6 14.5 reshape.500
  44.1 7.2 all-to-all-start
  51.6 2.7 copy.64
  55.5 143.5 %all-to-all-done = bf16[16,2,131072]{2,1,0:T(2,128)(2,1)} async-done(((bf16[16,2,131072]{2,1,0:T(2,128)(2,1)}), bf16[16,2,131072]{2,1,0:T(2,128)(2,1)}, u32[]{:S(2)}, u32[]{:S(2)}) %all-to-all-start) | async-done | bytes 8388640 | tf_op jit(solution)/shard_map/all_to_all | solution.py:15
  199.0 16.3 reshape.501
  215.3 12.2 fusion.32
  228.8 3.5 fusion.115
  232.4 3.9 fusion.118
  236.2 4.0 online-softmax.3
  241.2 5.2 fusion.117
  246.4 4.0 online-softmax.2
  251.3 5.1 fusion.116
  256.4 4.0 online-softmax.1
  261.5 4.2 online-softmax
  267.3 8.1 convolution_bitcast_fusion.1
  275.4 113.2 %reduce-scatter.12.cloned.1.call-done = f32[128,1,2048]{2,0,1:T(8,128)} async-done(((f32[2048,1,2048]{2,0,1:T(8,128)}), f32[128,1,2048]{2,0,1:T(8,128)}) %reduce-scatter.12.cloned.1.call-update) | async-done | bytes 1048592 | tf_op jit(solution)/shard_map/reduce_scatter | solution.py:172
  388.6 1.6 fusion.113
  391.5 1.7 add_convert_fusion.3
  393.9 2.6 convert_reduce_fusion.4
  396.6 67.0 %all-gather.4.cloned.1.call-done = bf16[2048,1,2048]{2,0,1:T(8,128)(2,1)} async-done(((bf16[128,1,2048]{2,0,1:T(8,128)(2,1)}), bf16[2048,1,2048]{2,0,1:T(8,128)(2,1)}) %all-gather.4.cloned.1.call-update) | async-done | bytes 8388624 | tf_op jit(solution)/shard_map/all_gather | solution.py:182
  463.6 10.5 fusion.15
  474.1 62.6 %all-gather.6.cloned.1.call-done = bf16[2048,1,2048]{2,0,1:T(8,128)(2,1)} async-done(((bf16[128,1,2048]{2,0,1:T(8,128)(2,1)}), bf16[2048,1,2048]{2,0,1:T(8,128)(2,1)}) %all-gather.6.cloned.1.call-update) | async-done | bytes 8388624 | tf_op jit(solution)/shard_map/all_gather | solution.py:208
  536.7 12.7 convert_reduce_fusion
  550.8 8.2 convolution_bitcast_fusion
  559.1 10.3 convert_bitcast_fusion.1
  569.5 99.9 %reduce-scatter.16.cloned.1.call-done = f32[128,1,2048]{2,0,1:T(8,128)} async-done(((f32[2048,1,2048]{2,0,1:T(8,128)}), f32[128,1,2048]{2,0,1:T(8,128)}) %reduce-scatter.16.cloned.1.call-update) | async-done | bytes 1048592 | tf_op jit(solution)/shard_map/reduce_scatter | solution.py:224
  669.4 2.2 multiply_reduce_fusion.4
  671.6 85.8 %reduce-scatter.14.cloned.1.call-done = bf16[128,1,2048]{2,0,1:T(8,128)(2,1)} async-done(((bf16[2048,1,2048]{2,0,1:T(8,128)(2,1)}), bf16[128,1,2048]{2,0,1:T(8,128)(2,1)}) %reduce-scatter.14.cloned.1.call-update) | async-done | bytes 524304 | tf_op jit(solution)/shard_map/reduce_scatter | solution.py:194
  757.4 2.5 fusion.112
  764.1 11.2 multiply_convert_fusion
  775.4 39.2 %copy.85 = bf16[2048,1,2048]{0,2,1:T(8,128)(2,1)} copy(bf16[2048,1,2048]{2,1,0:T(2,128)(2,1)} %reshape.501) | data formatting | bytes 16777216 | tf_op jit(solution)/shard_map/reshape | solution.py:141
  814.6 3.2 exponential_reduce_fusion
  823.1 9.6 multiply_convert_fusion.1
  833.0 5.9 fusion.46
  838.9 2.9 fusion.99
  841.8 2.8 fusion.102
  844.7 2.7 fusion.105
  848.3 9.5 multiply_reduce_fusion
  857.8 4.6 multiply_convert_fusion.3
  862.4 9.7 multiply_convert_fusion.2
  872.1 2.1 fusion.76
  874.2 3.3 fusion.78
  878.9 1.4 fusion.77
  884.2 1.7 convolution_add_fusion.2
  886.0 1.7 convolution_add_fusion.1
  887.7 2.8 fusion.57
  890.5 2.3 fusion.54
  894.0 1.7 copy.73
  895.7 8.3 fusion.39
  904.1 9.8 convert_bitcast_fusion
  914.8 73.7 %all-reduce = f32[8192]{0:T(1024)S(1)} all-reduce(f32[8192]{0:T(1024)S(1)} %broadcast_multiply_fusion.1), channel_id=10, replica_groups=mesh['group'=4,'dp'=2,'tensor'=16] {'group','dp','tensor'}, use_global_device_ids=true, to_apply=%region_38.39.clone | all-reduce | flops 8192 | bytes 65536
  989.1 1.8 convert_element_type.264
  990.9 1.8 convert_element_type.261
  993.1 1.7 convert_element_type.259
  994.8 45.6 %reduce-scatter.20.cloned.1.call-done = bf16[256,3,1,128]{3,0,1,2:T(8,128)(2,1)} async-done(((bf16[2048,3,1,128]{3,0,1,2:T(8,128)(2,1)}), bf16[256,3,1,128]{3,0,1,2:T(8,128)(2,1)}) %reduce-scatter.20.cloned.1.call-update) | async-done | bytes 196624 | tf_op jit(solution)/shard_map/reduce_scatter | solution.py:274
  1040.4 2.0 copy.75
  1042.3 89.8 %reduce-scatter.18.cloned.1.call-done = bf16[128,1,2048]{2,0,1:T(8,128)(2,1)} async-done(((bf16[2048,1,2048]{2,0,1:T(8,128)(2,1)}), bf16[128,1,2048]{2,0,1:T(8,128)(2,1)}) %reduce-scatter.18.cloned.1.call-update) | async-done | bytes 524304 | tf_op jit(solution)/shard_map/reduce_scatter | solution.py:256
  1132.2 1.4 convert_reduce_fusion.2
  1133.6 1.6 fusion.84
  1136.7 2.7 add_convert_fusion
  1139.4 707.3 %reduce-scatter.28.cloned.1.call-done = f32[16,8]{1,0:T(8,128)} async-done(((f32[2048,8]{1,0:T(8,128)}), f32[16,8]{1,0:T(8,128)}) %reduce-scatter.28.cloned.1.call-update) | async-done | bytes 528
  (244 shorter events, 40.2 us)
Async XLA Ops:
  7.2 529.5 %copy-start = (bf16[512,2048]{1,0:T(8,128)(2,1)S(1)}, bf16[512,2048]{1,0:T(8,128)(2,1)}, u32[]{:S(2)}) copy-start(bf16[512,2048]{1,0:T(8,128)(2,1)} %param.28) | copy-start | bytes 6291460
  44.1 10.1 copy-start.66
  44.1 11.4 copy-start.63
  44.1 154.9 %all-to-all-start = ((bf16[16,2,131072]{2,1,0:T(2,128)(2,1)}), bf16[16,2,131072]{2,1,0:T(2,128)(2,1)}, u32[]{:S(2)}, u32[]{:S(2)}) async-start(bf16[16,2,131072]{2,1,0:T(2,128)(2,1)} %reshape.500), calls=%async_computation | async-start | bytes 16777216 | tf_op jit(solution)/shard_map/all_to_all | solution.py:15
  51.3 337.2 %reduce-scatter.12.cloned.1.call-start = ((), (), s32[]{:S(2)}) async-start(), calls=%async_computation.10 | async-start | bytes 17825792 | tf_op jit(solution)/shard_map/reduce_scatter | solution.py:172
  54.8 196.5 %copy-start.35 = (s32[512]{0:T(512)}, s32[512]{0:T(512)S(1)}, u32[]{:S(2)}) copy-start(s32[512]{0:T(512)S(1)} %iota_add_fusion.2) | copy-start | bytes 6148
  54.8 186.3 %copy-start.33 = (s32[512]{0:T(512)}, s32[512]{0:T(512)S(1)}, u32[]{:S(2)}) copy-start(s32[512]{0:T(512)S(1)} %iota_add_fusion.1) | copy-start | bytes 6148
  55.5 172.1 %copy-start.56 = (f32[128]{0:T(128)}, f32[128]{0:T(128)S(1)}, u32[]{:S(2)}) copy-start(f32[128]{0:T(128)S(1)} %get-tuple-element.150) | copy-start | bytes 1540
  227.6 4.8 copy-start.12
  227.6 23.7 %copy-start.17 = (bf16[2048,1,128]{2,0,1:T(8,128)(2,1)}, bf16[2048,1,128]{2,0,1:T(8,128)(2,1)S(1)}, u32[]{:S(2)}) copy-start(bf16[2048,1,128]{2,0,1:T(8,128)(2,1)S(1)} %fusion.86) | copy-start | bytes 1572868
  260.4 6.8 copy-start.23
  275.3 116.1 %copy-start.29 = (f32[2048]{0:T(1024)S(1)}, f32[2048]{0:T(1024)}, u32[]{:S(2)}) copy-start(f32[2048]{0:T(1024)} %param.24) | copy-start | bytes 24580
  275.4 188.3 %all-gather.4.cloned.1.call-start = ((), (), s32[]{:S(2)}) async-start(), calls=%async_computation.11 | async-start | bytes 8912896 | tf_op jit(solution)/shard_map/all_gather | solution.py:182
  393.2 143.5 %all-gather.6.cloned.1.call-start = ((), (), s32[]{:S(2)}) async-start(), calls=%async_computation.13 | async-start | bytes 8912896 | tf_op jit(solution)/shard_map/all_gather | solution.py:208
  396.6 272.8 %reduce-scatter.16.cloned.1.call-start = ((), (), s32[]{:S(2)}) async-start(), calls=%async_computation.14 | async-start | bytes 17825792 | tf_op jit(solution)/shard_map/reduce_scatter | solution.py:224
  536.7 14.0 copy-start.70
  559.0 198.4 %reduce-scatter.14.cloned.1.call-start = ((), (), s32[]{:S(2)}) async-start(), calls=%async_computation.12 | async-start | bytes 8912896 | tf_op jit(solution)/shard_map/reduce_scatter | solution.py:194
  569.3 100.0 %copy-start.53 = (f32[128]{0:T(128)S(1)}, f32[128]{0:T(128)}, u32[]{:S(2)}) copy-start(f32[128]{0:T(128)} %copy-done.52) | copy-start | bytes 1540
  569.3 100.0 %copy-start.59 = (f32[128]{0:T(128)S(1)}, f32[128]{0:T(128)}, u32[]{:S(2)}) copy-start(f32[128]{0:T(128)} %copy-done.58) | copy-start | bytes 1540
  569.3 102.3 %copy-start.65 = (f32[128]{0:T(128)S(1)}, f32[128]{0:T(128)}, u32[]{:S(2)}) copy-start(f32[128]{0:T(128)} %copy-done.64) | copy-start | bytes 1540
  569.3 188.1 %copy-start.51 = (f32[2048]{0:T(1024)S(1)}, f32[2048]{0:T(1024)}, u32[]{:S(2)}) copy-start(f32[2048]{0:T(1024)} %param.29) | copy-start | bytes 24580
  569.4 190.6 %copy-start.15 = (bf16[128,1,2048]{2,0,1:T(8,128)(2,1)S(1)}, bf16[128,1,2048]{2,0,1:T(8,128)(2,1)}, u32[]{:S(2)}) copy-start(bf16[128,1,2048]{2,0,1:T(8,128)(2,1)} %get-tuple-element.133) | copy-start | bytes 1572868
  569.4 192.0 %copy-start.67 = (s32[8]{0:T(128)S(1)}, s32[8]{0:T(128)}, u32[]{:S(2)}) copy-start(s32[8]{0:T(128)} %param.17) | copy-start | bytes 100
  569.4 194.7 %copy-start.71 = (f32[512]{0:T(512)S(1)}, f32[512]{0:T(512)}, u32[]{:S(2)}) copy-start(f32[512]{0:T(512)} %param.27) | copy-start | bytes 6148
  569.4 263.6 %all-gather.8.cloned.1.call-start = ((), (), s32[]{:S(2)}) async-start(), calls=%async_computation.15 | async-start | bytes 8912896 | tf_op jit(solution)/shard_map/all_gather | solution.py:236
  760.0 15.4 copy-start.14
  760.0 15.4 copy-start.60
  761.1 228.0 %reduce-scatter.26.cloned.1.call-start = ((), (), s32[]{:S(2)}) async-start(), calls=%async_computation.20 | async-start | bytes 2359296 | tf_op jit(solution)/shard_map/reduce_scatter | solution.py:283
  775.4 39.2 %copy-start.48 = (f32[512]{0:T(512)S(1)}, f32[512]{0:T(512)}, u32[]{:S(2)}) copy-start(f32[512]{0:T(512)} %get-tuple-element.158) | copy-start | bytes 6148
  775.4 215.5 %reduce-scatter.24.cloned.1.call-start = ((), (), s32[]{:S(2)}) async-start(), calls=%async_computation.19 | async-start | bytes 2359296 | tf_op jit(solution)/shard_map/reduce_scatter | solution.py:280
  814.6 3.6 copy-start.50
  814.6 5.0 copy-start.5
  814.6 5.0 copy-start.49
  818.9 38.9 %copy-start.39 = (f32[512]{0:T(512)}, f32[512]{0:T(512)S(1)}, u32[]{:S(2)}) copy-start(f32[512]{0:T(512)S(1)} %get-tuple-element.164) | copy-start | bytes 6148
  818.9 43.5 %copy-start.37 = (f32[512]{0:T(512)}, f32[512]{0:T(512)S(1)}, u32[]{:S(2)}) copy-start(f32[512]{0:T(512)S(1)} %get-tuple-element.163) | copy-start | bytes 6148
  821.8 40.6 %copy-start.41 = (f32[512]{0:T(512)}, f32[512]{0:T(512)S(1)}, u32[]{:S(2)}) copy-start(f32[512]{0:T(512)S(1)} %get-tuple-element.165) | copy-start | bytes 6148
  821.8 40.6 %copy-start.43 = (f32[512]{0:T(512)}, f32[512]{0:T(512)S(1)}, u32[]{:S(2)}) copy-start(f32[512]{0:T(512)S(1)} %get-tuple-element.166) | copy-start | bytes 6148
  823.1 9.9 copy-start.24
  832.7 160.4 %reduce-scatter.22.cloned.1.call-start = ((), (), s32[]{:S(2)}) async-start(), calls=%async_computation.18 | async-start | bytes 589824 | tf_op jit(solution)/shard_map/reduce_scatter | solution.py:277
  833.0 14.4 copy-start.8
  838.9 8.5 copy-start.21
  838.9 8.5 copy-start.6
  841.8 5.6 copy-start.2
  841.8 6.5 copy-start.4
  841.8 6.5 copy-start.34
  841.8 6.5 copy-start.36
  872.1 5.4 copy-start.13
  872.1 6.8 copy-start.11
  874.2 6.0 copy-start.18
  885.9 4.5 slice-start
  892.8 147.6 %reduce-scatter.20.cloned.1.call-start = ((), (), s32[]{:S(2)}) async-start(), calls=%async_computation.17 | async-start | bytes 1769472 | tf_op jit(solution)/shard_map/reduce_scatter | solution.py:274
  904.0 228.1 %reduce-scatter.18.cloned.1.call-start = ((), (), s32[]{:S(2)}) async-start(), calls=%async_computation.16 | async-start | bytes 8912896 | tf_op jit(solution)/shard_map/reduce_scatter | solution.py:256
  913.9 218.2 %copy-start.9 = (bf16[128,1,2048]{2,0,1:T(8,128)(2,1)S(1)}, bf16[128,1,2048]{2,0,1:T(8,128)(2,1)}, u32[]{:S(2)}) copy-start(bf16[128,1,2048]{2,0,1:T(8,128)(2,1)} %param.15) | copy-start | bytes 1572868
  913.9 218.2 %copy-start.28 = (f32[2048]{0:T(1024)S(1)}, f32[2048]{0:T(1024)}, u32[]{:S(2)}) copy-start(f32[2048]{0:T(1024)} %param.18) | copy-start | bytes 24580
  913.9 218.2 %copy-start.46 = (f32[128]{0:T(128)S(1)}, f32[128]{0:T(128)}, u32[]{:S(2)}) copy-start(f32[128]{0:T(128)} %copy-done.45) | copy-start | bytes 1540
  914.0 219.6 %copy-start.69 = (f32[128]{0:T(128)S(1)}, f32[128]{0:T(128)}, u32[]{:S(2)}) copy-start(f32[128]{0:T(128)} %copy-done.68) | copy-start | bytes 1540
  914.0 219.6 %copy-start.55 = (f32[128]{0:T(128)S(1)}, f32[128]{0:T(128)}, u32[]{:S(2)}) copy-start(f32[128]{0:T(128)} %copy-done.54) | copy-start | bytes 1540
  914.0 221.2 %copy-start.30 = (f32[2048]{0:T(1024)S(1)}, f32[2048]{0:T(1024)}, u32[]{:S(2)}) copy-start(f32[2048]{0:T(1024)} %get-tuple-element.132) | copy-start | bytes 24580
  914.0 221.2 %copy-start.31 = (f32[2048]{0:T(1024)S(1)}, f32[2048]{0:T(1024)}, u32[]{:S(2)}) copy-start(f32[2048]{0:T(1024)} %get-tuple-element.121) | copy-start | bytes 24580
  914.0 221.2 %copy-start.32 = (f32[2048]{0:T(1024)S(1)}, f32[2048]{0:T(1024)}, u32[]{:S(2)}) copy-start(f32[2048]{0:T(1024)} %get-tuple-element.125) | copy-start | bytes 24580
  914.0 222.7 %copy-start.16 = (bf16[128,1,2048]{2,0,1:T(8,128)(2,1)S(1)}, bf16[128,1,2048]{2,0,1:T(8,128)(2,1)}, u32[]{:S(2)}) copy-start(bf16[128,1,2048]{2,0,1:T(8,128)(2,1)} %get-tuple-element.133) | copy-start | bytes 1572868
  914.0 222.7 %copy-start.61 = (f32[128]{0:T(128)S(1)}, f32[128]{0:T(128)}, u32[]{:S(2)}) copy-start(f32[128]{0:T(128)} %copy-done.60) | copy-start | bytes 1540
  914.0 932.7 %reduce-scatter.28.cloned.1.call-start = ((), (), s32[]{:S(2)}) async-start(), calls=%async_computation.21 | async-start | bytes 1056768
  993.1 859.5 %copy-start.1 = (bf16[512,2048]{1,0:T(8,128)(2,1)S(1)}, bf16[512,2048]{1,0:T(8,128)(2,1)}, u32[]{:S(2)}) copy-start(bf16[512,2048]{1,0:T(8,128)(2,1)} %param.28) | copy-start | bytes 6291460
  (25 other events, 44.4 us)
Sparse Core Ops, SparseCore 0:
  275.5 113.0 reduce-scatter.11
  393.3 70.2 all-gather.3
  466.4 70.3 all-gather.5
  559.1 110.1 reduce-scatter.15
  672.6 84.7 reduce-scatter.13
  761.2 69.9 all-gather.7
  833.7 56.8 reduce-scatter.25
  892.9 59.3 reduce-scatter.23
  954.7 38.4 reduce-scatter.21
  995.5 44.7 reduce-scatter.19
  1044.2 87.9 reduce-scatter.17
  1136.8 709.8 reduce-scatter.27
